TPU v7x, 128 devices: a whole 4x4x4 slice. The times are simulated.
128 devices in a mesh: row: 8 (over x, y_hi), col: 16 (over y_lo, z, core).
Axes of the slice: x: 4, y: 4 (y_hi: 2, y_lo: 2; y = y_hi * 2 + y_lo), z: 4, core: 2. Of those that a mesh axis runs over, the one named last changes fastest.
Arguments:
- train_inputs: bfloat16 [512, 8192], P(('row', 'col')), may hold values from -6 to 6
- train_grads: bfloat16 [512, 8192], P(('row', 'col')), may hold values from -6 to 6
- query_inputs: bfloat16 [256, 8192], P(('row', 'col')), may hold values from -6 to 6
- query_grads: bfloat16 [256, 8192], P(('row', 'col')), may hold values from -6 to 6
- input_basis: bfloat16 [8192, 8192], P('row', 'col'), may hold values from -0.0625 to 0.0625
- output_basis: bfloat16 [8192, 8192], P('col', 'row'), may hold values from -0.0625 to 0.0625
- eigenvalues: float32 [8192, 8192], P('row', 'col'), may hold values from 0.5 to 5
- query_starts: int32 [16], replicated, may hold values from 0 to 255, as said below
- query_ends: int32 [16], replicated, may hold values from 1 to 256, as said below
Outputs:
- scores: float32 [16, 512], replicated
Inputs may be any that keep to these rules, and one draw needn't show every extreme that they name: Query q covers the query rows query_starts[q] <= r < query_ends[q]: a nonempty span of at most 128 rows that lies inside one aligned block of 128 rows (rows k * 128 to (k + 1) * 128 - 1); spans of different queries may intersect or share a block. `query_ends`: see query_starts.
All inputs are finite; a program needn't handle non-finite values.
Results may differ from a plain program's by a relative error of at most 0.005.
Values may be sent and summed in bfloat16 or wider, within the bound.
A program may use at most 64 MiB of HBM per device.

v0:
```python
import math
import jax
import jax.numpy as jnp
from jax import lax
from jax.sharding import Mesh
from jax.sharding import PartitionSpec as P

D_IN = 8192
D_OUT = 8192
QBLOCK = 128
COL = ("col_0", "col_1", "col_2")
ROW = ("row_0", "row_1")
ROW_COL = ("row_0", "row_1", "col_0", "col_1", "col_2")
damping = 0.1


def laid_out(parts, dim):
    parts = jnp.moveaxis(parts, 0, dim)
    dims = parts.shape
    return parts.reshape(*dims[:dim], dims[dim] * dims[dim + 1], *dims[dim + 2 :])


def gather_together(arrays, axis, dims):
    line = jnp.concatenate([a.reshape(-1) for a in arrays])
    lines, at, gathered = (lax.all_gather(line, axis), 0, [])
    for a, dim in zip(arrays, dims):
        parts = lines[:, at : at + a.size].reshape(-1, *a.shape)
        gathered.append(laid_out(parts, dim))
        at += a.size
    return tuple(gathered)


def by_axis(value, axes):
    for axis in axes:
        value = lax.psum(value, axis)
    return value


def shards(
    train_inputs,
    train_grads,
    query_inputs,
    query_grads,
    input_basis,
    output_basis,
    eigenvalues,
    query_starts,
    query_ends,
):
    grouped = gather_together((train_inputs, query_inputs), COL, (0, 0))
    train_in, query_in = (
        lax.all_to_all(grouped[0], ROW, split_axis=1, concat_axis=0, tiled=True),
        lax.all_to_all(grouped[1], ROW, split_axis=1, concat_axis=0, tiled=True),
    )
    spread = (
        lax.all_to_all(train_grads, COL, split_axis=1, concat_axis=0, tiled=True),
        lax.all_to_all(query_grads, COL, split_axis=1, concat_axis=0, tiled=True),
    )
    train_out, query_out = gather_together((spread[0], spread[1]), ROW, (0, 0))
    train_in_part = jnp.dot(train_in, input_basis, preferred_element_type=jnp.float32)
    query_in_part = jnp.dot(query_in, input_basis, preferred_element_type=jnp.float32)
    train_out_part = jnp.dot(train_out, output_basis, preferred_element_type=jnp.float32)
    query_out_part = jnp.dot(query_out, output_basis, preferred_element_type=jnp.float32)
    in_sums = lax.psum((train_in_part, query_in_part), ROW)
    out_sums = lax.psum((train_out_part, query_out_part), COL)
    train_in_rot = in_sums[0].astype(jnp.bfloat16)
    query_in_rot = in_sums[1].astype(jnp.bfloat16)
    train_grad_rot = out_sums[0].astype(jnp.bfloat16)
    query_grad_rot = out_sums[1].astype(jnp.bfloat16)
    grads_wide = train_grad_rot.astype(jnp.float32)
    denominator = eigenvalues + damping

    def per_query(span):
        span_start, span_end = span
        block_top = span_start // QBLOCK * QBLOCK
        grad_rows = lax.dynamic_slice_in_dim(query_grad_rot, block_top, QBLOCK, 0)
        input_rows = lax.dynamic_slice_in_dim(query_in_rot, block_top, QBLOCK, 0)
        positions = block_top + jnp.arange(QBLOCK, dtype=jnp.int32)
        inside = (positions >= span_start) & (positions < span_end)
        grad_rows = jnp.where(inside[:, None], grad_rows, jnp.zeros((), grad_rows.dtype))
        outer_sum = lax.dot_general(
            grad_rows, input_rows, (((0,), (0,)), ((), ())), preferred_element_type=jnp.float32
        )
        scaled = (outer_sum / denominator).astype(jnp.bfloat16)
        paired = lax.dot_general(
            train_in_rot, scaled, (((1,), (1,)), ((), ())), preferred_element_type=jnp.float32
        )
        return jnp.sum(grads_wide * paired, axis=1)

    partial_scores = lax.map(per_query, (query_starts, query_ends))
    totals = by_axis(partial_scores, ROW_COL)
    return totals * (1.0 / math.sqrt(D_IN * D_OUT * QBLOCK))


def solution(mesh):
    split = Mesh(mesh.devices.reshape(4, 2, 2, 4, 2), ("row_0", "row_1", "col_0", "col_1", "col_2"))
    placed = (
        P(ROW_COL, None),
        P(ROW_COL, None),
        P(ROW_COL, None),
        P(ROW_COL, None),
        P(ROW, COL),
        P(COL, ROW),
        P(ROW, COL),
        P(),
        P(),
    )
    return jax.shard_map(shards, mesh=split, in_specs=placed, out_specs=P(), check_vma=False)
```

profile of v0, /device:TPU:1, one launch (start us, length us, event | category | flops | bytes accessed | tf_op | source)
XLA Modules:
  0.0 458.6 jit_solution(13673715249605043826)
XLA Ops:
  8.9 13.6 %all_to_all.70 = bf16[2,16,512]{2,0,1:T(2,128)(2,1)S(1)} all-to-all(bf16[2,16,512]{2,0,1:T(2,128)(2,1)} %bitcast.54), channel_id=1, replica_groups=mesh['row_0'=4,'row_1'=2,'col_0'=2,'col_1'=4,'col_2'=2] {'col_0','col_1'..., dimensions={1} | all-to-all | bytes 65536 | tf_op jit(solution)/shard_map/all_to_all | solution.py:57
  22.6 3.7 all-to-all-start
  26.2 3.2 broadcast_add_fusion
  32.2 31.4 %all-gather = bf16[393216]{0:T(1024)(128)(2,1)S(1)} all-gather(bf16[49152]{0:T(1024)(128)(2,1)S(1)} %pad_maximum_fusion), channel_id=2, replica_groups=mesh['row_0'=4,'row_1'=2,'col_0'=2,'col_1'=4,'col_2'=2] {'row_0','row_1'}, dimensions={0}, use_global_device_ids=true | all-gather | bytes 884736 | tf_op jit(solution)/shard_map/all_gather | solution.py:25
  70.1 4.5 all-to-all-start.2
  85.9 6.6 %all-to-all-start.3 = ((bf16[64,8,1024]{2,0,1:T(8,128)(2,1)}), bf16[64,8,1024]{2,0,1:T(8,128)(2,1)}, u32[]{:S(2)}, u32[]{:S(2)}) async-start(bf16[64,8,1024]{2,0,1:T(8,128)(2,1)} %copy.22), calls=%async_computation.3 | async-start | bytes 2097152 | tf_op jit(solution)/shard_map/all_to_all | solution.py:52
  92.6 74.4 %all-reduce.4 = (bf16[256,1024]{1,0:T(8,128)(2,1)}, bf16[512,1024]{1,0:T(8,128)(2,1)}) all-reduce(f32[256,1024]{1,0:T(8,128)} %fusion.15, f32[512,1024]{1,0:T(8,128)S(1)} %fusion.18), channel_id=1, replica_groups=mesh['row_0'=4,'row_1'=2,'col_0'=2,'col_1'=4,'col_2'=2] {'col_0','col_1'..., use_global_device_ids=true, to_apply=%region_0.0 | all-reduce | flops 786432 | bytes 4718592 | tf_op jit(solution)/shard_map/psum | solution.py:65
  171.0 3.3 fusion.17
  174.3 81.4 %all-reduce.5 = (bf16[256,512]{1,0:T(8,128)(2,1)}, bf16[512,512]{1,0:T(8,128)(2,1)}) all-reduce(f32[256,512]{1,0:T(8,128)} %fusion.16, f32[512,512]{1,0:T(8,128)} %fusion.17), channel_id=1, replica_groups=mesh['row_0'=4,'row_1'=2,'col_0'=2,'col_1'=4,'col_2'=2] {'row_0','row_1'}, use_global_device_ids=true, to_apply=%region_1.0 | all-reduce | flops 393216 | bytes 2359296 | tf_op jit(solution)/shard_map/psum | solution.py:64
  255.7 127.2 %while.12 = (s32[]{:T(128)}, f32[16,512]{1,0:T(8,128)S(1)}, s32[16]{0:T(128)S(1)}, s32[16]{0:T(128)S(1)}, bf16[256,1024]{1,0:T(8,128)(2,1)}, /*index=5*/bf16[256...) while((s32[]{:T(128)}, f32[16,512]{1,0:T(8,128)S(1)}, ...), condition=%wide.region_6.7_spmd, body=%wide.region_4.6_spmd.sunk | while | flops 673316864 | bytes 5119617 | solution.py:90
  260.6 2.9 fusion.35
  276.6 2.9 fusion.35
  284.5 2.9 fusion.35
  292.5 2.9 fusion.35
  308.4 2.9 fusion.35
  324.3 2.9 fusion.35
  340.2 2.9 fusion.35
  356.1 2.9 fusion.35
  372.0 2.9 fusion.35
  383.0 11.8 %psum.67 = f32[16,512]{1,0:T(8,128)S(1)} all-reduce(f32[16,512]{1,0:T(8,128)S(1)} %get-tuple-element.119), channel_id=1, replica_groups=mesh['row_0'=4,'row_1'=2,'col_0'=2,'col_1'=4,'col_2'=2] {'row_0'}, use_global_device_ids=true, to_apply=%region_7.8 | all-reduce | flops 8192 | bytes 65536 | tf_op jit(solution)/shard_map/psum | solution.py:35
  394.8 7.5 %psum.68 = f32[16,512]{1,0:T(8,128)S(1)} all-reduce(f32[16,512]{1,0:T(8,128)S(1)} %psum.67), channel_id=1, replica_groups=mesh['row_0'=4,'row_1'=2,'col_0'=2,'col_1'=4,'col_2'=2] {'row_1'}, use_global_device_ids=true, to_apply=%region_8.9 | all-reduce | flops 8192 | bytes 65536 | tf_op jit(solution)/shard_map/psum | solution.py:35
  402.3 6.6 %psum.69 = f32[16,512]{1,0:T(8,128)S(1)} all-reduce(f32[16,512]{1,0:T(8,128)S(1)} %psum.68), channel_id=1, replica_groups=mesh['row_0'=4,'row_1'=2,'col_0'=2,'col_1'=4,'col_2'=2] {'col_0'}, use_global_device_ids=true, to_apply=%region_9.10 | all-reduce | flops 8192 | bytes 65536 | tf_op jit(solution)/shard_map/psum | solution.py:35
  409.0 18.8 %psum.70 = f32[16,512]{1,0:T(8,128)S(1)} all-reduce(f32[16,512]{1,0:T(8,128)S(1)} %psum.69), channel_id=1, replica_groups=mesh['row_0'=4,'row_1'=2,'col_0'=2,'col_1'=4,'col_2'=2] {'col_1'}, use_global_device_ids=true, to_apply=%region_10.11 | all-reduce | flops 8192 | bytes 65536 | tf_op jit(solution)/shard_map/psum | solution.py:35
  427.7 23.4 %psum.71 = f32[16,512]{1,0:T(8,128)S(1)} all-reduce(f32[16,512]{1,0:T(8,128)S(1)} %psum.70), channel_id=1, replica_groups=mesh['row_0'=4,'row_1'=2,'col_0'=2,'col_1'=4,'col_2'=2] {'col_2'}, use_global_device_ids=true, to_apply=%region_11.12 | all-reduce | flops 8192 | bytes 65536 | tf_op jit(solution)/shard_map/psum | solution.py:35
  (114 shorter events, 88.1 us)
Async XLA Ops:
  6.5 68.1 %copy-start = (bf16[512,1024]{1,0:T(8,128)(2,1)S(1)}, bf16[512,1024]{1,0:T(8,128)(2,1)}, u32[]{:S(2)}) copy-start(bf16[512,1024]{1,0:T(8,128)(2,1)} %param.16) | copy-start | bytes 3145732
  6.5 58.5 %all-gather.4.cloned.1.call-start = ((), (), s32[]{:S(2)}) async-start(), calls=%async_computation.4 | async-start | bytes 1671168 | tf_op jit(solution)/shard_map/all_gather | solution.py:25
  22.6 9.6 %all-to-all-start = ((bf16[4,16,512]{2,0,1:T(4,128)(2,1)}), bf16[4,16,512]{2,0,1:T(4,128)(2,1)S(1)}, u32[]{:S(2)}, u32[]{:S(2)}) async-start(bf16[4,16,512]{2,0,1:T(4,128)(2,1)} %bitcast.51), calls=%async_computation | async-start | bytes 131072 | tf_op jit(solution)/shard_map/all_to_all | solution.py:56
  63.9 1.1 copy-start.3
  66.8 3.3 copy-start.1
  70.1 6.3 %slice-start = ((bf16[8,49152]{1,0:T(8,128)(2,1)}), bf16[8,16384]{1,0:T(8,128)(2,1)S(1)}, s32[]{:S(2)}) async-start(bf16[8,49152]{1,0:T(8,128)(2,1)} %copy-done.3), calls=%async_computation.5 | async-start | bytes 524288 | tf_op jit(solution)/shard_map/slice | solution.py:27
  70.1 15.8 %all-to-all-start.2 = ((bf16[32,8,1024]{2,0,1:T(8,128)(2,1)}), bf16[32,8,1024]{2,0,1:T(8,128)(2,1)}, u32[]{:S(2)}, u32[]{:S(2)}) async-start(bf16[32,8,1024]{2,0,1:T(8,128)(2,1)} %copy.21), calls=%async_computation.2 | async-start | bytes 1048576 | tf_op jit(solution)/shard_map/all_to_all | solution.py:53
  77.2 2.5 copy-start.2
  85.9 85.1 %all-to-all-start.3 = ((bf16[64,8,1024]{2,0,1:T(8,128)(2,1)}), bf16[64,8,1024]{2,0,1:T(8,128)(2,1)}, u32[]{:S(2)}, u32[]{:S(2)}) async-start(bf16[64,8,1024]{2,0,1:T(8,128)(2,1)} %copy.22), calls=%async_computation.3 | async-start | bytes 2097152 | tf_op jit(solution)/shard_map/all_to_all | solution.py:52
  171.0 84.7 %copy-start.4 = (s32[16]{0:T(128)S(1)}, s32[16]{0:T(128)}, u32[]{:S(2)}) copy-start(s32[16]{0:T(128)} %param.18) | copy-start | bytes 196
  171.0 84.7 %copy-start.5 = (s32[16]{0:T(128)S(1)}, s32[16]{0:T(128)}, u32[]{:S(2)}) copy-start(s32[16]{0:T(128)} %param.19) | copy-start | bytes 196
Sparse Core Ops, SparseCore 0:
  9.1 38.4 all-gather.3
where the time goes:
time: 461 us; the launch traced here: 459 us
  blocking collectives  269 us (58%)
  matrix products  56.8 us (12%)
  loops' own time  40.5 us (9%)
  local copies, waits for them, and re-layouts  37.2 us (8%)
  other arithmetic  24.1 us (5%)
  starting transfers between devices  14.8 us (3%)
  between operations  13.5 us (3%)
    psum x1, blocking collectives, shards(): in_sums = lax.psum((train_in_part, query_in_part), ROW)  81.4 us
    psum x1, blocking collectives, shards(): out_sums = lax.psum((train_out_part, query_out_part), COL)  74.4 us
    psum x5, blocking collectives, by_axis(): value = lax.psum(value, axis)  68.1 us
    dot_general x16, matrix products, per_query(): lax.dot_general(train_in_rot, scaled, (((1,), (1,)), ((), ())), preferred...  46.7 us
    another operation x1, loops' own time, shards(): partial_scores = lax.map(per_query, (query_starts, query_ends))  40.5 us
    all_gather x1, blocking collectives, gather_together(): lines, at, gathered = (lax.all_gather(line, axis), 0, [])  31.4 us
    and x16, other arithmetic, per_query(): inside = (positions >= span_start) & (positions < span_end)  19.6 us
    dynamic_slice x32, local copies, waits for them, and re-layouts, shards(): partial_scores = lax.map(per_query, (query_starts, query_ends))  19.4 us
  transfers between devices with their start and end apart: 4, of which 1 were waited for; matrix products, arithmetic and copies ran while one was open for 4% of the time, Pallas kernels for 0%

commit v1 on v0

--- a/solution.py
+++ b/solution.py
@@ -4,6 +4,7 @@
 from jax import lax
 from jax.sharding import Mesh
 from jax.sharding import PartitionSpec as P
+from jax.lax import all_gather
 
 D_IN = 8192
 D_OUT = 8192
@@ -32,7 +33,7 @@
 
 def by_axis(value, axes):
     for axis in axes:
-        value = lax.psum(value, axis)
+        value = all_gather(value, axis).sum(axis=0)
     return value
 
 

time: 461 us -> 444 us (0.963)
  blocking collectives: 269 us -> 252 us
    psum x5 -> x0, blocking collectives: 68.1 us -> none  [by_axis(): value = lax.psum(value, axis)]
    all_gather x0 -> x5, blocking collectives: none -> 51 us  [by_axis(): value = all_gather(value, axis).sum(axis=0)]
where the time goes in v1:
time: 444 us; the launch traced here: 442 us
  blocking collectives  252 us (57%)
  matrix products  56.8 us (13%)
  loops' own time  40.5 us (9%)
  local copies, waits for them, and re-layouts  37.2 us (8%)
  other arithmetic  24.2 us (5%)
  starting transfers between devices  14.8 us (3%)
  between operations  13.5 us (3%)
    psum x1, blocking collectives, shards(): in_sums = lax.psum((train_in_part, query_in_part), ROW)  81.4 us
    psum x1, blocking collectives, shards(): out_sums = lax.psum((train_out_part, query_out_part), COL)  74.4 us
    all_gather x5, blocking collectives, by_axis(): value = all_gather(value, axis).sum(axis=0)  51 us
    dot_general x16, matrix products, per_query(): lax.dot_general(train_in_rot, scaled, (((1,), (1,)), ((), ())), preferred...  46.7 us
    another operation x1, loops' own time, shards(): partial_scores = lax.map(per_query, (query_starts, query_ends))  40.5 us
    all_gather x1, blocking collectives, gather_together(): lines, at, gathered = (lax.all_gather(line, axis), 0, [])  31.4 us
    and x16, other arithmetic, per_query(): inside = (positions >= span_start) & (positions < span_end)  19.6 us
    dynamic_slice x32, local copies, waits for them, and re-layouts, shards(): partial_scores = lax.map(per_query, (query_starts, query_ends))  19.4 us
  transfers between devices with their start and end apart: 4, of which 1 were waited for; matrix products, arithmetic and copies ran while one was open for 4% of the time, Pallas kernels for 0%

profile of v1, /device:TPU:1, one launch (start us, length us, event | category | flops | bytes accessed | tf_op | source)
XLA Modules:
  0.0 441.5 jit_solution(11337243910885903842)
XLA Ops:
  8.9 13.6 %all_to_all.70 = bf16[2,16,512]{2,0,1:T(2,128)(2,1)S(1)} all-to-all(bf16[2,16,512]{2,0,1:T(2,128)(2,1)} %bitcast.64), channel_id=1, replica_groups=mesh['row_0'=4,'row_1'=2,'col_0'=2,'col_1'=4,'col_2'=2] {'col_0','col_1'..., dimensions={1} | all-to-all | bytes 65536 | tf_op jit(solution)/shard_map/all_to_all | solution.py:58
  22.6 3.7 all-to-all-start
  26.2 3.2 broadcast_add_fusion
  32.2 31.4 %all-gather = bf16[393216]{0:T(1024)(128)(2,1)S(1)} all-gather(bf16[49152]{0:T(1024)(128)(2,1)S(1)} %pad_maximum_fusion), channel_id=2, replica_groups=mesh['row_0'=4,'row_1'=2,'col_0'=2,'col_1'=4,'col_2'=2] {'row_0','row_1'}, dimensions={0}, use_global_device_ids=true | all-gather | bytes 884736 | tf_op jit(solution)/shard_map/all_gather | solution.py:26
  70.1 4.5 %all-to-all-start.2 = ((bf16[32,8,1024]{2,0,1:T(8,128)(2,1)}), bf16[32,8,1024]{2,0,1:T(8,128)(2,1)}, u32[]{:S(2)}, u32[]{:S(2)}) async-start(bf16[32,8,1024]{2,0,1:T(8,128)(2,1)} %copy.26), calls=%async_computation.2 | async-start | bytes 1048576 | tf_op jit(solution)/shard_map/all_to_all | solution.py:54
  85.9 6.6 %all-to-all-start.3 = ((bf16[64,8,1024]{2,0,1:T(8,128)(2,1)}), bf16[64,8,1024]{2,0,1:T(8,128)(2,1)}, u32[]{:S(2)}, u32[]{:S(2)}) async-start(bf16[64,8,1024]{2,0,1:T(8,128)(2,1)} %copy.27), calls=%async_computation.3 | async-start | bytes 2097152 | tf_op jit(solution)/shard_map/all_to_all | solution.py:53
  92.6 74.4 %all-reduce.4 = (bf16[256,1024]{1,0:T(8,128)(2,1)}, bf16[512,1024]{1,0:T(8,128)(2,1)}) all-reduce(f32[256,1024]{1,0:T(8,128)} %fusion.15, f32[512,1024]{1,0:T(8,128)S(1)} %fusion.18), channel_id=1, replica_groups=mesh['row_0'=4,'row_1'=2,'col_0'=2,'col_1'=4,'col_2'=2] {'col_0','col_1'..., use_global_device_ids=true, to_apply=%region_0.0 | all-reduce | flops 786432 | bytes 4718592 | tf_op jit(solution)/shard_map/psum | solution.py:66
  171.0 3.3 fusion.17
  174.3 81.4 %all-reduce.5 = (bf16[256,512]{1,0:T(8,128)(2,1)}, bf16[512,512]{1,0:T(8,128)(2,1)}) all-reduce(f32[256,512]{1,0:T(8,128)} %fusion.16, f32[512,512]{1,0:T(8,128)} %fusion.17), channel_id=1, replica_groups=mesh['row_0'=4,'row_1'=2,'col_0'=2,'col_1'=4,'col_2'=2] {'row_0','row_1'}, use_global_device_ids=true, to_apply=%region_1.0 | all-reduce | flops 393216 | bytes 2359296 | tf_op jit(solution)/shard_map/psum | solution.py:65
  255.7 127.2 %while.12 = (s32[]{:T(128)}, f32[16,512]{1,0:T(8,128)S(1)}, s32[16]{0:T(128)S(1)}, s32[16]{0:T(128)S(1)}, bf16[256,1024]{1,0:T(8,128)(2,1)}, /*index=5*/bf16[256...) while((s32[]{:T(128)}, f32[16,512]{1,0:T(8,128)S(1)}, ...), condition=%wide.region_6.7_spmd, body=%wide.region_4.6_spmd.sunk | while | flops 673316864 | bytes 5119617 | solution.py:91
  260.6 2.9 fusion.35
  276.6 2.9 fusion.35
  284.5 2.9 fusion.35
  292.5 2.9 fusion.35
  308.4 2.9 fusion.35
  324.3 2.9 fusion.35
  340.2 2.9 fusion.35
  356.1 2.9 fusion.35
  372.0 2.9 fusion.35
  383.0 9.1 %all-gather.2 = f32[64,512]{1,0:T(8,128)S(1)} all-gather(f32[16,512]{1,0:T(8,128)S(1)} %get-tuple-element.119), channel_id=4, replica_groups=mesh['row_0'=4,'row_1'=2,'col_0'=2,'col_1'=4,'col_2'=2] {'row_0'}, dimensions={0}, use_global_device_ids=true | all-gather | bytes 163840 | tf_op jit(solution)/shard_map/all_gather | solution.py:36
  392.1 4.9 %all-gather.3 = f32[32,512]{1,0:T(8,128)S(1)} all-gather(f32[16,512]{1,0:T(8,128)S(1)} %reduce_sum.57), channel_id=5, replica_groups=mesh['row_0'=4,'row_1'=2,'col_0'=2,'col_1'=4,'col_2'=2] {'row_1'}, dimensions={0}, use_global_device_ids=true | all-gather | bytes 98304 | tf_op jit(solution)/shard_map/all_gather | solution.py:36
  397.0 3.4 all-gather.4
  400.5 13.7 %all-gather.5 = f32[64,512]{1,0:T(8,128)S(1)} all-gather(f32[16,512]{1,0:T(8,128)S(1)} %reduce_sum.59), channel_id=7, replica_groups=mesh['row_0'=4,'row_1'=2,'col_0'=2,'col_1'=4,'col_2'=2] {'col_1'}, dimensions={0}, use_global_device_ids=true | all-gather | bytes 163840 | tf_op jit(solution)/shard_map/all_gather | solution.py:36
  414.2 19.8 %all-gather.6 = f32[32,512]{1,0:T(8,128)S(1)} all-gather(f32[16,512]{1,0:T(8,128)S(1)} %reduce_sum.60), channel_id=8, replica_groups=mesh['row_0'=4,'row_1'=2,'col_0'=2,'col_1'=4,'col_2'=2] {'col_2'}, dimensions={0}, use_global_device_ids=true | all-gather | bytes 98304 | tf_op jit(solution)/shard_map/all_gather | solution.py:36
  (119 shorter events, 88.1 us)
Async XLA Ops:
  6.5 68.1 %copy-start = (bf16[512,1024]{1,0:T(8,128)(2,1)S(1)}, bf16[512,1024]{1,0:T(8,128)(2,1)}, u32[]{:S(2)}) copy-start(bf16[512,1024]{1,0:T(8,128)(2,1)} %param.16) | copy-start | bytes 3145732
  6.5 58.5 %all-gather.9.cloned.1.call-start = ((), (), s32[]{:S(2)}) async-start(), calls=%async_computation.4 | async-start | bytes 1671168 | tf_op jit(solution)/shard_map/all_gather | solution.py:26
  22.6 9.6 %all-to-all-start = ((bf16[4,16,512]{2,0,1:T(4,128)(2,1)}), bf16[4,16,512]{2,0,1:T(4,128)(2,1)S(1)}, u32[]{:S(2)}, u32[]{:S(2)}) async-start(bf16[4,16,512]{2,0,1:T(4,128)(2,1)} %bitcast.61), calls=%async_computation | async-start | bytes 131072 | tf_op jit(solution)/shard_map/all_to_all | solution.py:57
  63.9 1.1 copy-start.3
  66.8 3.3 copy-start.1
  70.1 6.3 %slice-start = ((bf16[8,49152]{1,0:T(8,128)(2,1)}), bf16[8,16384]{1,0:T(8,128)(2,1)S(1)}, s32[]{:S(2)}) async-start(bf16[8,49152]{1,0:T(8,128)(2,1)} %copy-done.3), calls=%async_computation.5 | async-start | bytes 524288 | tf_op jit(solution)/shard_map/slice | solution.py:28
  70.1 15.8 %all-to-all-start.2 = ((bf16[32,8,1024]{2,0,1:T(8,128)(2,1)}), bf16[32,8,1024]{2,0,1:T(8,128)(2,1)}, u32[]{:S(2)}, u32[]{:S(2)}) async-start(bf16[32,8,1024]{2,0,1:T(8,128)(2,1)} %copy.26), calls=%async_computation.2 | async-start | bytes 1048576 | tf_op jit(solution)/shard_map/all_to_all | solution.py:54
  77.2 2.5 copy-start.2
  85.9 85.1 %all-to-all-start.3 = ((bf16[64,8,1024]{2,0,1:T(8,128)(2,1)}), bf16[64,8,1024]{2,0,1:T(8,128)(2,1)}, u32[]{:S(2)}, u32[]{:S(2)}) async-start(bf16[64,8,1024]{2,0,1:T(8,128)(2,1)} %copy.27), calls=%async_computation.3 | async-start | bytes 2097152 | tf_op jit(solution)/shard_map/all_to_all | solution.py:53
  171.0 84.7 %copy-start.4 = (s32[16]{0:T(128)S(1)}, s32[16]{0:T(128)}, u32[]{:S(2)}) copy-start(s32[16]{0:T(128)} %param.18) | copy-start | bytes 196
  171.0 84.7 %copy-start.5 = (s32[16]{0:T(128)S(1)}, s32[16]{0:T(128)}, u32[]{:S(2)}) copy-start(s32[16]{0:T(128)} %param.19) | copy-start | bytes 196
Sparse Core Ops, SparseCore 0:
  9.1 38.4 all-gather.8
